TPU v7x, 32 devices: a whole 2x2x4 slice. The times are simulated.
32 devices in a mesh: row: 8 (over y, x, core), col: 4 (over z).
Axes of the slice: x: 2, y: 2, z: 4, core: 2. Of those that a mesh axis runs over, the one named last changes fastest.
Arguments:
- inverse_rows: float32 [16384, 16384], P('col', 'row'), may hold values from -0.5 to 0.5
- panels: float32 [4, 16384, 256], P('col', 'row'), may hold values from -0.75 to 0.75
- diag_inverse: float32 [2, 256, 256], replicated, may hold values from -12 to 12
- pattern: int32 [2, 64], replicated, may hold values 0 or 1
- owner_slot: int32 [2], replicated, may hold values from 0 to 3, as said below
Outputs:
- inverse_column: float32 [2, 16384, 256], P(None, 'row')
- inverse_row: float32 [2, 256, 16384], P(None, None, 'col')
- diag_block: float32 [2, 256, 256], replicated
Inputs may be any that keep to these rules, and one draw needn't show every extreme that they name: `owner_slot`: the two supernodes' panels lie in two different slots, one of them the last slot.
All inputs are finite; a program needn't handle non-finite values.
Results may differ from a plain program's by a relative error of at most 0.0001.
Values sent between devices are 32-bit elements; how exact they have to be, the bound alone decides.
A program may use at most 128 MiB of HBM per device.

v0:
```python
import jax
import jax.numpy as jnp
from jax import lax
from jax.sharding import PartitionSpec as P


def from_root(array, axis, root):
    mine = lax.axis_index(axis) == root
    return lax.psum(jnp.where(mine, array, jnp.zeros_like(array)), axis)


def block_mask(pattern_row, start_block, count_blocks, width):
    live = lax.dynamic_slice_in_dim(pattern_row, start_block, count_blocks, 0).astype(jnp.float32)
    return jnp.repeat(live, width)


def shards(inverse_rows, panels, diag_inverse, pattern, owner_slot):
    n_rows = lax.axis_size("row")
    n_cols = lax.axis_size("col")
    row_index = lax.axis_index("row")
    col_index = lax.axis_index("col")
    rows_here = panels.shape[1]
    cols_here = inverse_rows.shape[0]
    width = panels.shape[2]
    blocks = pattern.shape[1]
    source_col = row_index * n_cols // n_rows
    start_row = row_index * rows_here - source_col * cols_here
    masked_list = []
    colmask_list = []
    for number in range(2):
        mask_rows = block_mask(
            pattern[number], row_index * (blocks // n_rows), blocks // n_rows, width
        )
        mask_cols = block_mask(
            pattern[number], col_index * (blocks // n_cols), blocks // n_cols, width
        )
        held = from_root(panels[0], "col", owner_slot[number])
        masked_list.append(mask_rows[:, None] * held)
        colmask_list.append(mask_cols)
    masked_all = jnp.stack(masked_list)
    colmask_all = jnp.stack(colmask_list)
    partial_value = jnp.einsum(
        "ij,sjw->siw", inverse_rows, masked_all, precision=lax.Precision.HIGHEST
    )
    column_total = lax.psum(partial_value, "row")
    column = -(colmask_all[:, :, None] * column_total)
    piece = lax.dynamic_slice_in_dim(column, start_row, rows_here, 1)
    lower = from_root(piece, "col", source_col)
    inner = jnp.einsum("sjw,sjv->swv", masked_all, lower, precision=lax.Precision.HIGHEST)
    diagonal = diag_inverse - lax.psum(inner, "row")
    return (lower, jnp.swapaxes(column, 1, 2), diagonal)


def solution(mesh):
    in_specs = (P("col", "row"), P("col", "row", None), P(), P(), P())
    out_specs = (P(None, "row", None), P(None, None, "col"), P())
    return jax.shard_map(shards, mesh=mesh, in_specs=in_specs, out_specs=out_specs, check_vma=False)
```

profile of v0, /device:TPU:7, one launch (start us, length us, event | category | flops | bytes accessed | tf_op | source)
XLA Modules:
  0.0 588.9 jit_solution(14428068676685210212)
XLA Ops:
  7.2 0.0 all-reduce.12.cloned.1.call-start
  7.2 1.3 fusion.17
  9.8 1.9 copy.8
  11.8 0.0 copy-start.2
  11.8 2.5 select_bitcast_fusion.1
  14.3 0.0 all-reduce.12.cloned.1.call-update
  14.3 0.0 all-reduce.6.cloned.1.call-start
  14.4 0.1 fusion.11
  14.5 0.1 broadcast_bitcast_fusion.3
  14.6 0.1 fusion.13
  14.6 0.1 broadcast_bitcast_fusion.2
  14.7 155.8 %all-reduce.12.cloned.1.call-done = (f32[2048,256]{0,1:T(8,128)}, f32[2048,256]{0,1:T(8,128)}) async-done(((f32[2048,256]{0,1:T(8,128)}, f32[2048,256]{0,1:T(8,128)}), (f32[2048,256]{0,1:T(8,128)}, f32[2048,256]{0,1:T(8,128)})) %all-reduce.12.cloned.1.call-update) | async-done | bytes 4194320 | tf_op jit(solution)/shard_map/psum | solution.py:9
  170.5 2.6 multiply_bitcast_fusion
  173.1 1.3 copy-done
  174.4 59.4 %fusion.2 = f32[2,4096,256]{1,2,0:T(8,128)} fusion(f32[4096,2048]{1,0:T(8,128)} %param.5, f32[1,2048,256]{1,2,0:T(8,128)S(1)} %get-tuple-element.14, f32[1,2048,256]{1,2,0:T(8,128)S(1)} %get-tuple-element.15), kind=kOutput, calls=%fused_computation.3 | convolution fusion | flops 51540656128 | bytes 46137344 | tf_op jit(solution)/shard_map/ij,sjw->siw/dot_general | solution.py:42
  233.8 0.0 all-reduce.6.cloned.1.call-update
  233.8 0.0 all-reduce.8.cloned.1.call-start
  233.9 0.1 fusion.7
  234.0 0.1 broadcast_bitcast_fusion.1
  234.1 0.1 broadcast_bitcast_fusion
  234.2 123.5 %all-reduce.6.cloned.1.call-done = f32[2,4096,256]{1,2,0:T(8,128)} async-done(((f32[2,4096,256]{1,2,0:T(8,128)}), f32[2,4096,256]{1,2,0:T(8,128)}) %all-reduce.6.cloned.1.call-update) | async-done | bytes 8388624 | tf_op jit(solution)/shard_map/psum | solution.py:45
  357.8 4.3 multiply_negate_fusion
  362.1 2.3 dynamic-slice_select_fusion
  364.4 0.0 all-reduce.8.cloned.1.call-update
  364.4 0.0 all-reduce.10.cloned.1.call-start
  364.5 156.6 %all-reduce.8.cloned.1.call-done = f32[2,2048,256]{1,2,0:T(8,128)} async-done(((f32[2,2048,256]{1,2,0:T(8,128)}), f32[2,2048,256]{1,2,0:T(8,128)}) %all-reduce.8.cloned.1.call-update) | async-done | bytes 4194320 | tf_op jit(solution)/shard_map/psum | solution.py:9
  521.1 7.6 %fusion.5 = f32[2,256,256]{2,1,0:T(8,128)} fusion(f32[2,2048,256]{1,2,0:T(8,128)} %all-reduce.8.cloned.1.call-done, f32[1,2048,256]{1,2,0:T(8,128)S(1)} %get-tuple-element.14, f32[1,2048,256]{1,2,0:T(8,128)} %copy-done), kind=kOutput, calls=%fused_computation.6 | convolution fusion | flops 3222274048 | bytes 8912896 | tf_op jit(solution)/shard_map/sjw,sjv->swv/dot_general | solution.py:49
  528.7 0.0 all-reduce.10.cloned.1.call-update
  528.7 8.3 %fusion.19 = f32[2,256,4096]{2,1,0:T(8,128)} fusion(f32[2,4096,256]{1,2,0:T(8,128)} %all-reduce.6.cloned.1.call-done, f32[2,4096]{1,0:T(2,128)S(1)} %pad_maximum_fusion.3), kind=kLoop, calls=%fused_computation.32 | loop fusion | flops 4194304 | bytes 16809984 | tf_op jit(solution)/shard_map/transpose | solution.py:51
  537.0 5.4 copy.11
  542.4 38.1 %all-reduce.10.cloned.1.call-done = f32[2,256,256]{2,1,0:T(8,128)} async-done(((f32[2,256,256]{2,1,0:T(8,128)}), f32[2,256,256]{2,1,0:T(8,128)}) %all-reduce.10.cloned.1.call-update) | async-done | bytes 524304 | tf_op jit(solution)/shard_map/psum | solution.py:50
  580.5 1.9 sub.12
  (10 shorter events, 0.1 us)
Async XLA Ops:
  7.2 163.4 %all-reduce.12.cloned.1.call-start = ((), (), s32[]{:S(2)}) async-start(), calls=%async_computation.3 | async-start | bytes 8388608 | tf_op jit(solution)/shard_map/psum | solution.py:9
  11.8 2.6 copy-start.2
  14.3 343.4 %all-reduce.6.cloned.1.call-start = ((), (), s32[]{:S(2)}) async-start(), calls=%async_computation | async-start | bytes 16777216 | tf_op jit(solution)/shard_map/psum | solution.py:45
  173.1 1.3 copy-start
  233.8 287.3 %all-reduce.8.cloned.1.call-start = ((), (), s32[]{:S(2)}) async-start(), calls=%async_computation.1 | async-start | bytes 8388608 | tf_op jit(solution)/shard_map/psum | solution.py:9
  364.4 216.1 %all-reduce.10.cloned.1.call-start = ((), (), s32[]{:S(2)}) async-start(), calls=%async_computation.2 | async-start | bytes 1048576 | tf_op jit(solution)/shard_map/psum | solution.py:50
  537.0 43.5 %copy-start.1 = (f32[2,256,256]{2,1,0:T(8,128)S(1)}, f32[2,256,256]{2,1,0:T(8,128)}, u32[]{:S(2)}) copy-start(f32[2,256,256]{2,1,0:T(8,128)} %param.7) | copy-start | bytes 1572868
Sparse Core Ops, SparseCore 0:
  14.4 156.0 all-reduce.11
  233.9 123.7 all-reduce.5
  364.5 156.5 all-reduce.7
  528.8 51.6 all-reduce.9
where the time goes:
time: 593 us; the launch traced here: 589 us
  waiting for transfers between devices  474 us (80%)
  matrix products  67 us (11%)
  other arithmetic  22.1 us (4%)
  between operations  15.2 us (3%)
  local copies, waits for them, and re-layouts  10.3 us (2%)
    psum x2, waiting for transfers between devices, from_root(): return lax.psum(jnp.where(mine, array, jnp.zeros_like(array)), axis)  312 us
    psum x1, waiting for transfers between devices, shards(): column_total = lax.psum(partial_value, 'row')  124 us
    dot_general x1, matrix products, shards(): jnp.einsum('ij,sjw->siw', inverse_rows, masked_all, precision=lax.Precisi...  59.4 us
    psum x1, waiting for transfers between devices, shards(): diagonal = diag_inverse - lax.psum(inner, 'row')  38.1 us
  transfers between devices with their start and end apart: 4, of which 4 were waited for; matrix products, arithmetic and copies ran while one was open for 2% of the time, Pallas kernels for 0%

commit v1 on v0

v1 whole, which is shorter than its diff:
```python
import functools

import jax
import jax.numpy as jnp
from jax import lax
from jax.experimental import pallas as pl
from jax.experimental.pallas import tpu as pltpu
from jax.sharding import PartitionSpec as P

MESH = pl.DeviceIdType.MESH
F32 = jnp.float32
BF16 = jnp.bfloat16
CHUNKS = 8
TILES = 16


def halves(x):
    high = x.astype(BF16)
    return high, (x - high.astype(F32)).astype(BF16)


def dot3(a, b):
    (ah, al), (bh, bl) = a, b
    out = jnp.dot(ah, bh, preferred_element_type=F32)
    out += jnp.dot(ah, bl, preferred_element_type=F32)
    out += jnp.dot(al, bh, preferred_element_type=F32)
    return out


def kernel(
    n_rows, n_cols,
    a_ref, own_last, own_other, sign_ref, dinv_ref,
    y_out, low_out, diag_out,
    bf, bh, bl, plus, minus, part, y, low, abuf, dpart, dsum, *rest,
):
    bits = n_rows.bit_length() - 1
    rs_buf, d_buf = rest[:bits], rest[bits:2 * bits]
    (last_s, last_r, plus_s, plus_r, minus_s, minus_r, rs_s, rs_r, ag_s, ag_r,
     zl_s, zr_s, z_r, a_sem, o_sem) = rest[2 * bits:]
    r = lax.axis_index("row")
    c = lax.axis_index("col")
    width = bf.shape[2]
    depth = bf.shape[1]
    rows = y.shape[1]
    ch = depth // CHUNKS
    tm = rows // TILES
    end = n_cols - 1
    core = lax.rem(r, 2)
    left, right = {"col": c - 1}, {"col": c + 1}

    def bit_of(j):
        if j == 0:
            return 1
        return (1 << j) + core * ((1 << (bits - j)) - (1 << j))

    value = [lax.rem(lax.div(r, bit_of(j)), 2) for j in range(bits)]
    partner = [r + (1 - 2 * value[j]) * bit_of(j) for j in range(bits)]

    def starts(total):
        out = [0]
        for j in range(bits):
            out.append(out[-1] + value[j] * (total >> (j + 1)))
        return out

    def span(start, size):
        return pl.ds(pl.multiple_of(start, 8), size)

    def chunk(k):
        return span(k * ch, ch)

    def remote(src, dst, send, recv, where):
        return pltpu.make_async_remote_copy(
            src_ref=src, dst_ref=dst, send_sem=send, recv_sem=recv,
            device_id=where, device_id_type=MESH,
        )

    def a_copy(g):
        t = lax.rem(g, TILES)
        start = lax.rem(t * tm + (1 - value[0]) * (rows // 2), rows)
        slot = lax.rem(g, 2)
        return start, slot, pltpu.make_async_copy(
            a_ref.at[span(start, tm), :], abuf.at[slot], a_sem.at[slot]
        )

    def multiply(s, t):
        g = s * TILES + t
        start, slot, copy = a_copy(g)

        @pl.when(g + 1 < 2 * TILES)
        def _():
            a_copy(g + 1)[2].start()

        copy.wait()
        total = None
        step = min(512, depth)
        for k in range(0, depth, step):
            a = halves(abuf[slot, :, k:k + step])
            term = dot3(a, (bh[s, k:k + step, :], bl[s, k:k + step, :]))
            total = term if total is None else total + term
        part[s, span(start, tm), :] = total

    def loop(low_, high_, body):
        def step(i, carry):
            body(i)
            return carry
        lax.fori_loop(low_, high_, step, 0)

    def split(s, k):
        high, rest_ = halves(bf[s, chunk(k), :])
        bh[s, chunk(k), :] = high
        bl[s, chunk(k), :] = rest_

    def last_copy(k, src):
        return remote(src, bf.at[0, chunk(k), :], last_s.at[k], last_r.at[k], left)

    def plus_copy(k, src):
        return remote(src, plus.at[chunk(k), :], plus_s.at[k], plus_r.at[k], right)

    def minus_copy(k, src):
        return remote(src, minus.at[chunk(k), :], minus_s.at[k], minus_r.at[k], left)

    def first_phase(k):
        here = chunk(k)

        @pl.when(c == end)
        def _():
            bf[0, here, :] = own_last[here, :]

        @pl.when(c < end)
        def _():
            last_copy(k, bf.at[0, here, :]).wait_recv()

        @pl.when((c < end) & (c > 0))
        def _():
            last_copy(k, bf.at[0, here, :]).start()

        split(0, k)

        @pl.when(c == 0)
        def _():
            plus[here, :] = own_other[here, :]

        @pl.when(c > 0)
        def _():
            plus_copy(k, plus.at[here, :]).wait_recv()
            plus[here, :] = plus[here, :] + own_other[here, :]

        @pl.when((c > 0) & (c < end))
        def _():
            plus_copy(k, plus.at[here, :]).start()

    def second_phase(k):
        here = chunk(k)

        @pl.when(c < end - 1)
        def _():
            minus_copy(k, minus.at[here, :]).wait_recv()
            arrived = minus[here, :]
            bf[1, here, :] = plus[here, :] + arrived
            minus[here, :] = arrived + own_other[here, :]

        @pl.when((c < end - 1) & (c > 0))
        def _():
            minus_copy(k, minus.at[here, :]).start()

        @pl.when(c >= end - 1)
        def _():
            bf[1, here, :] = plus[here, :]

        @pl.when((c == end - 1) & (c > 0))
        def _():
            minus_copy(k, own_other.at[here, :]).start()

        split(1, k)

    def reduce_events(s, src, bufs, dst, total, finish):
        start = starts(total)
        size = [total >> j for j in range(bits + 1)]

        def rs(j):
            away = start[j] + (1 - value[j]) * size[j + 1]
            return remote(src.at[span(away, size[j + 1]), :], bufs[j],
                          rs_s.at[s, j], rs_r.at[s, j], {"row": partner[j]})

        def ag(j):
            mine = span(start[j + 1], size[j + 1])
            return remote(dst.at[mine, :], dst.at[mine, :],
                          ag_s.at[s, j], ag_r.at[s, j], {"row": partner[j]})

        def add(j):
            rs(j).wait()
            mine = size[j + 1]
            piece = min(mine, 128)

            def body(i):
                here = span(start[j + 1] + i * piece, piece)
                src[here, :] = src[here, :] + bufs[j][span(i * piece, piece), :]
            loop(0, mine // piece, body)

        def event(i):
            if i == 0:
                rs(0).start()
            elif i < bits:
                add(i - 1)
                rs(i).start()
            elif i == bits:
                add(bits - 1)
                finish(start[bits], size[bits])
                ag(bits - 1).start()
            else:
                j = 2 * bits - i
                ag(j).wait()
                if j > 0:
                    ag(j - 1).start()
        return [functools.partial(event, i) for i in range(2 * bits + 1)]

    def finish_column(s, start, size):
        piece = min(size, width, 128)

        def body(i):
            at = start + i * piece
            block = lax.div(c * rows + at, width)
            here = span(at, piece)
            y[s, here, :] = sign_ref[s, block] * part[s, here, :]
        loop(0, size // piece, body)

    source = lax.div(r * n_cols, n_rows)
    own_start = r * depth - source * rows

    def z_copy(s, k, src, way):
        sem = zl_s if way < 0 else zr_s
        return remote(src, low.at[s, chunk(k), :], sem.at[s, k], z_r.at[s, k],
                      left if way < 0 else right)

    def z_send(s, k, src):
        @pl.when((c <= source) & (c > 0))
        def _():
            z_copy(s, k, src, -1).start()

        @pl.when((c >= source) & (c < end))
        def _():
            z_copy(s, k, src, 1).start()

    def z_root(s):
        @pl.when(c == source)
        def _():
            def send(k):
                z_send(s, k, y.at[s, span(own_start + k * ch, ch), :])
            loop(0, CHUNKS, send)

            def keep(k):
                low[s, chunk(k), :] = y[s, span(own_start + k * ch, ch), :]
            loop(0, CHUNKS, keep)

    def z_relay(s, k):
        @pl.when(c != source)
        def _():
            z_copy(s, k, low.at[s, chunk(k), :], 1).wait_recv()
            z_send(s, k, low.at[s, chunk(k), :])

    def y_copy(s):
        return pltpu.make_async_copy(y.at[s], y_out.at[s], o_sem.at[s])

    def low_copy(s):
        return pltpu.make_async_copy(low.at[s], low_out.at[s], o_sem.at[2 + s])

    def inner(s, k):
        b = halves(bf[s, chunk(k), :].T)
        here = pl.ds(s * width, width)
        dpart[here, :] += dot3(b, halves(low[s, chunk(k), :]))

    barrier = pltpu.get_barrier_semaphore()
    for j in range(bits):
        pl.semaphore_signal(barrier, inc=1, device_id={"row": partner[j]}, device_id_type=MESH)

    @pl.when(c > 0)
    def _():
        pl.semaphore_signal(barrier, inc=1, device_id=left, device_id_type=MESH)

    @pl.when(c < end)
    def _():
        pl.semaphore_signal(barrier, inc=1, device_id=right, device_id_type=MESH)

    beside = lax.div(c + end - 1, end) + lax.div(2 * end - 1 - c, end)
    pl.semaphore_wait(barrier, bits + beside)

    a_copy(0)[2].start()

    @pl.when(c == end)
    def _():
        loop(0, CHUNKS, lambda k: last_copy(k, own_last.at[chunk(k), :]).start())

    @pl.when(c == 0)
    def _():
        loop(0, CHUNKS, lambda k: plus_copy(k, own_other.at[chunk(k), :]).start())

    loop(0, CHUNKS, first_phase)

    first = reduce_events(0, part.at[0], [b.at[0] for b in rs_buf], y.at[0], rows,
                          functools.partial(finish_column, 0))
    second = reduce_events(1, part.at[1], [b.at[1] for b in rs_buf], y.at[1], rows,
                           functools.partial(finish_column, 1))

    def finish_diag(start, size):
        here = span(start, size)
        dsum[here, :] = dpart[here, :]

    third = reduce_events(2, dpart, d_buf, dsum, 2 * width, finish_diag)

    def both(k):
        second_phase(k)
        loop(0, 4, lambda i: multiply(0, 4 * k + i))

    loop(0, 2, both)
    first[0]()
    loop(2, 4, both)
    todo = list(first[1:])
    for k in range(4, CHUNKS):
        second_phase(k)
        if todo:
            todo.pop(0)()
    loop(0, 4, lambda t: multiply(1, t))
    if todo:
        todo.pop(0)()
    loop(4, 8, lambda t: multiply(1, t))
    second[0]()
    for event in todo:
        event()
    z_root(0)
    y_copy(0).start()
    loop(8, 16, lambda t: multiply(1, t))
    rest_events = second[1:]
    done = 0
    for i, event in enumerate(rest_events):
        event()
        upto = CHUNKS * (i + 1) // len(rest_events)
        for k in range(done, upto):
            z_relay(0, k)
        done = upto
    z_root(1)
    y_copy(1).start()
    low_copy(0).start()
    dpart[...] = jnp.zeros_like(dpart)
    loop(0, CHUNKS, lambda k: inner(0, k))

    def tail(k):
        z_relay(1, k)
        inner(1, k)
    loop(0, CHUNKS, tail)
    low_copy(1).start()
    for event in third:
        event()
    diag_out[...] = dinv_ref[...] - dsum[...]

    def drain(k):
        here = chunk(k)

        @pl.when(c > 0)
        def _():
            last_copy(k, own_last.at[here, :]).wait_send()

        @pl.when(c < end)
        def _():
            plus_copy(k, plus.at[here, :]).wait_send()

        @pl.when((c < end) & (c > 0))
        def _():
            minus_copy(k, minus.at[here, :]).wait_send()

        for s in range(2):
            src = low.at[s, here, :]

            @pl.when((c <= source) & (c > 0))
            def _():
                z_copy(s, k, src, -1).wait_send()

            @pl.when((c >= source) & (c < end))
            def _():
                z_copy(s, k, src, 1).wait_send()
    loop(0, CHUNKS, drain)
    for s in range(2):
        y_copy(s).wait()
        low_copy(s).wait()


def exchange(n_rows, n_cols, a, own_last, own_other, sign, dinv):
    rows, depth = a.shape
    width = own_last.shape[1]
    bits = n_rows.bit_length() - 1
    vmem = pl.BlockSpec(memory_space=pltpu.VMEM)
    anywhere = pl.BlockSpec(memory_space=pl.ANY)
    dma = pltpu.SemaphoreType.DMA
    n = CHUNKS
    return pl.pallas_call(
        functools.partial(kernel, n_rows, n_cols),
        out_shape=(
            jax.ShapeDtypeStruct((2, rows, width), F32),
            jax.ShapeDtypeStruct((2, depth, width), F32),
            jax.ShapeDtypeStruct((2 * width, width), F32),
        ),
        in_specs=[anywhere, vmem, vmem, pl.BlockSpec(memory_space=pltpu.SMEM), vmem],
        out_specs=(anywhere, anywhere, vmem),
        scratch_shapes=[
            pltpu.VMEM((2, depth, width), F32),
            pltpu.VMEM((2, depth, width), BF16),
            pltpu.VMEM((2, depth, width), BF16),
            pltpu.VMEM((depth, width), F32),
            pltpu.VMEM((depth, width), F32),
            pltpu.VMEM((2, rows, width), F32),
            pltpu.VMEM((2, rows, width), F32),
            pltpu.VMEM((2, depth, width), F32),
            pltpu.VMEM((2, rows // TILES, depth), F32),
            pltpu.VMEM((2 * width, width), F32),
            pltpu.VMEM((2 * width, width), F32),
            *[pltpu.VMEM((2, rows >> (j + 1), width), F32) for j in range(bits)],
            *[pltpu.VMEM((2 * width >> (j + 1), width), F32) for j in range(bits)],
            dma((n,)), dma((n,)), dma((n,)), dma((n,)), dma((n,)), dma((n,)),
            dma((3, bits)), dma((3, bits)), dma((3, bits)), dma((3, bits)),
            dma((2, n)), dma((2, n)), dma((2, n)),
            dma((2,)), dma((4,)),
        ],
        compiler_params=pltpu.CompilerParams(
            collective_id=0, has_side_effects=True, vmem_limit_bytes=66_000_000
        ),
    )(a, own_last, own_other, sign, dinv)


def shards(inverse_rows, panels, diag_inverse, pattern, owner_slot):
    n_rows = lax.axis_size("row")
    n_cols = lax.axis_size("col")
    row_index = lax.axis_index("row")
    col_index = lax.axis_index("col")
    width = panels.shape[2]
    blocks_here = pattern.shape[1] // n_rows
    flip = (owner_slot[0] != n_cols - 1).astype(jnp.int32)
    order = (flip, 1 - flip)
    live = jnp.stack([lax.dynamic_index_in_dim(pattern, o, 0, keepdims=False) for o in order])
    live = live.astype(F32)
    mask = lax.dynamic_slice_in_dim(live, row_index * blocks_here, blocks_here, 1)
    mask = jnp.repeat(mask, width, axis=1)[:, :, None]
    own_last = mask[0] * panels[0]
    mine = owner_slot[order[1]] == col_index
    own_other = jnp.where(mine, mask[1] * panels[0], 0.0)
    dinv = jnp.concatenate(
        [lax.dynamic_index_in_dim(diag_inverse, o, 0, keepdims=False) for o in order]
    )
    y, low, diag = exchange(n_rows, n_cols, inverse_rows, own_last, own_other, -live, dinv)

    def back(x):
        return jnp.stack([lax.dynamic_index_in_dim(x, o, 0, keepdims=False) for o in order])
    return back(low), jnp.swapaxes(back(y), 1, 2), back(diag.reshape(2, width, width))


def solution(mesh):
    in_specs = (P("col", "row"), P("col", "row", None), P(), P(), P())
    out_specs = (P(None, "row", None), P(None, None, "col"), P())
    return jax.shard_map(shards, mesh=mesh, in_specs=in_specs, out_specs=out_specs, check_vma=False)
```

time: 593 us -> 382 us (0.64)
  waiting for transfers between devices: 474 us -> 0 us
  Pallas kernels: 0 us -> 346 us
  matrix products: 67 us -> 0 us
  between operations: 15.2 us -> 2.01 us
  other arithmetic: 22.1 us -> 12 us
  local copies, waits for them, and re-layouts: 10.3 us -> 17.1 us
    psum x4 -> x0, waiting for transfers between devices: 474 us -> none  [the longest x2 312 us: from_root(): return lax.psum(jnp.where(mine, array, jnp.zeros_like(array)), axis)]
    pallas_call x0 -> x1, Pallas kernels: none -> 346 us  [exchange(): pl.pallas_call(functools.partial(kernel, n_rows, n_cols), out_shape=(jax....]
    dot_general x2 -> x0, matrix products: 67 us -> none  [the longest x1 59.4 us: shards(): jnp.einsum('ij,sjw->siw', inverse_rows, masked_all, precision=lax.Precisi...]
  transfers between devices with their start and end apart: 4 -> 0, of which waited for: 4 -> 0; matrix products, arithmetic and copies ran while one was open for 2% -> 0% of each run, Pallas kernels for 0% -> 0%
where the time goes in v1:
time: 382 us; the launch traced here: 377 us
  Pallas kernels  346 us (91%)
  local copies, waits for them, and re-layouts  17.1 us (4%)
  other arithmetic  12 us (3%)
    pallas_call x1, Pallas kernels, exchange(): pl.pallas_call(functools.partial(kernel, n_rows, n_cols), out_shape=(jax....  346 us
    unnamed x10, local copies, waits for them, and re-layouts  10.6 us

profile of v1, /device:TPU:7, one launch (start us, length us, event | category | flops | bytes accessed | tf_op | source)
XLA Modules:
  0.0 377.0 jit_solution(8103047955949095471)
XLA Ops:
  1.3 1.2 dynamic_slice.43
  3.2 0.8 constant_dynamic-slice_fusion.8
  3.9 0.6 fusion.1.sign_ref
  4.5 0.1 constant_dynamic-slice_fusion.6
  4.6 0.1 broadcast_bitcast_fusion
  4.7 1.1 dynamic-slice_bitcast_fusion.1
  5.8 0.8 pad_maximum_fusion.1.dinv_ref
  6.6 3.6 fusion
  10.2 345.9 %shard_map.76 = (f32[2,4096,256]{2,1,0:T(8,128)}, f32[2,2048,256]{2,1,0:T(8,128)}, f32[512,256]{1,0:T(8,128)}) custom-call(f32[4096,2048]{1,0:T(8,128)} %a_ref.1, f32[2048,256]{1,0:T(8,128)} %get-tuple-element.17.own_last, f32[2048,256]{1,0:T(8,128)} %get-tuple-element.16.own_other, f32[2,64]{1,0:T(2,128)} %fusion.1.sign_ref, ...), custom_call_target="tpu_custom_call" | custom-call | tf_op jit(solution)/shard_map/pallas_call | solution.py:394
  356.1 0.0 slice-start
  356.1 2.7 constant_dynamic-slice_fusion.5
  358.8 0.0 copy-start
  358.8 0.0 slice-start.1
  358.8 2.4 pad_maximum_fusion
  361.2 0.0 copy-done
  361.2 0.0 slice-done
  361.2 1.6 slice-done.1
  362.8 0.7 constant_dynamic-slice_fusion.3
  363.5 3.8 maximum_bitcast_fusion
  367.2 8.9 %copy.8 = f32[2,256,4096]{2,1,0:T(8,128)} copy(f32[2,256,4096]{1,2,0:T(8,128)} %maximum_bitcast_fusion) | data formatting | bytes 16777216
  376.1 0.8 pad_maximum_fusion.2
  (6 shorter events, 0.1 us)
Async XLA Ops:
  356.1 5.2 %slice-start = ((s8[8388608]{0:T(1024)(128)(4,1)}), s8[4194304]{0:T(1024)(128)(4,1)S(1)}, s32[]{:S(2)}) async-start(s8[8388608]{0:T(1024)(128)(4,1)} %bitcast.25), calls=%async_computation | async-start | bytes 8388608
  358.8 2.4 copy-start
  358.8 4.0 %slice-start.1 = ((s8[8388608]{0:T(1024)(128)(4,1)}), s8[4194304]{0:T(1024)(128)(4,1)S(1)}, s32[]{:S(2)}) async-start(s8[8388608]{0:T(1024)(128)(4,1)} %bitcast.25), calls=%async_computation.1 | async-start | bytes 8388608

commit v2 on v1

v2 whole, which is shorter than its diff:
```python
import functools

import jax
import jax.numpy as jnp
from jax import lax
from jax.experimental import pallas as pl
from jax.experimental.pallas import tpu as pltpu
from jax.sharding import PartitionSpec as P

MESH = pl.DeviceIdType.MESH
F32 = jnp.float32
BF16 = jnp.bfloat16
CHUNKS = 16
TILES = 16


def halves(x):
    high = x.astype(BF16)
    return high, (x - high.astype(F32)).astype(BF16)


def dot3(a, b):
    (ah, al), (bh, bl) = a, b
    out = jnp.dot(ah, bh, preferred_element_type=F32)
    out += jnp.dot(ah, bl, preferred_element_type=F32)
    out += jnp.dot(al, bh, preferred_element_type=F32)
    return out


def weave(one, two):
    keyed = [((i + 0.5) / len(x), n, f) for n, x in enumerate((one, two)) for i, f in enumerate(x)]
    return [f for _, _, f in sorted(keyed, key=lambda item: item[:2])]


def kernel(
    n_rows, n_cols,
    a_ref, panel, scale_ref, sign_ref, dinv_ref,
    y_out, low_out, diag_out,
    bf, bh, bl, plus, minus, part, y, low, abuf, turned, dpart, dsum, *rest,
):
    bits = n_rows.bit_length() - 1
    rs_buf, d_buf = rest[:bits], rest[bits:2 * bits]
    (plus_s, plus_r, minus_s, minus_r, rs_s, rs_r, ag_s, ag_r,
     zl_s, zr_s, z_r, a_sem, t_sem, o_sem) = rest[2 * bits:]
    r = lax.axis_index("row")
    c = lax.axis_index("col")
    width = bf.shape[2]
    depth = bf.shape[1]
    rows = y.shape[1]
    ch = depth // CHUNKS
    tm = rows // TILES
    strip = rows // 4
    end = n_cols - 1
    core = lax.rem(r, 2)
    left, right = {"col": c - 1}, {"col": c + 1}

    def bit_of(j):
        if j == 0:
            return 1
        return (1 << j) + core * ((1 << (bits - j)) - (1 << j))

    value = [lax.rem(lax.div(r, bit_of(j)), 2) for j in range(bits)]
    partner = [r + (1 - 2 * value[j]) * bit_of(j) for j in range(bits)]

    def span(start, size):
        return pl.ds(pl.multiple_of(start, 8), size)

    def chunk(k):
        return span(k * ch, ch)

    def remote(src, dst, send, recv, where):
        return pltpu.make_async_remote_copy(
            src_ref=src, dst_ref=dst, send_sem=send, recv_sem=recv,
            device_id=where, device_id_type=MESH,
        )

    def loop(low_, high_, body):
        def step(i, carry):
            body(i)
            return carry
        lax.fori_loop(low_, high_, step, 0)

    def a_copy(g):
        t = lax.rem(g, TILES)
        quarter = lax.div(t, TILES // 4)
        half = (1 - value[0]) + lax.rem(quarter, 2) * (2 * value[0] - 1)
        start = (lax.div(quarter, 2) * strip + half * (rows // 2)
                 + lax.rem(t, TILES // 4) * tm)
        slot = lax.rem(g, 2)
        return start, slot, pltpu.make_async_copy(
            a_ref.at[span(start, tm), :], abuf.at[slot], a_sem.at[slot]
        )

    def multiply(s, t):
        g = s * TILES + t
        start, slot, copy = a_copy(g)

        @pl.when(g + 1 < 2 * TILES)
        def _():
            a_copy(g + 1)[2].start()

        copy.wait()
        total = None
        step = min(512, depth)
        for k in range(0, depth, step):
            a = halves(abuf[slot, :, k:k + step])
            term = dot3(a, (bh[s, k:k + step, :], bl[s, k:k + step, :]))
            total = term if total is None else total + term
        part[s, span(start, tm), :] = total

    def plus_copy(s, k):
        ref = plus.at[s, chunk(k), :]
        return remote(ref, ref, plus_s.at[s, k], plus_r.at[s, k], right)

    def minus_copy(s, k):
        ref = minus.at[s, chunk(k), :]
        return remote(ref, ref, minus_s.at[s, k], minus_r.at[s, k], left)

    def own(s, k):
        block = lax.div(r * depth + k * ch, width)
        return scale_ref[s, block] * panel[chunk(k), :]

    total_chunks = 2 * CHUNKS

    def panel_step(j):
        up = j - c

        @pl.when((up >= 0) & (up < total_chunks))
        def _():
            s, k = lax.div(up, CHUNKS), lax.rem(up, CHUNKS)

            @pl.when(c > 0)
            def _():
                plus_copy(s, k).wait_recv()
                plus[s, chunk(k), :] = plus[s, chunk(k), :] + own(s, k)

            @pl.when(c == 0)
            def _():
                plus[s, chunk(k), :] = own(s, k)

            @pl.when(c < end)
            def _():
                plus_copy(s, k).start()

        down = j - (end - c)

        @pl.when((down >= 0) & (down < total_chunks))
        def _():
            s, k = lax.div(down, CHUNKS), lax.rem(down, CHUNKS)

            @pl.when(c < end)
            def _():
                minus_copy(s, k).wait_recv()
                minus[s, chunk(k), :] = minus[s, chunk(k), :] + own(s, k)

            @pl.when(c == end)
            def _():
                minus[s, chunk(k), :] = own(s, k)

            @pl.when(c > 0)
            def _():
                minus_copy(s, k).start()

        at = j - end

        @pl.when(at >= 0)
        def _():
            s, k = lax.div(at, CHUNKS), lax.rem(at, CHUNKS)
            x = (plus[s, chunk(k), :] + minus[s, chunk(k), :]) - own(s, k)
            bf[s, chunk(k), :] = x
            high, rest_ = halves(x)
            bh[s, chunk(k), :] = high
            bl[s, chunk(k), :] = rest_

    def reduce_events(g, src, bufs, dst, apart, offset, first_size, finish):
        size = [None] + [first_size >> j for j in range(bits)]
        start = [None, value[0] * apart + offset]
        for j in range(1, bits):
            start.append(start[-1] + value[j] * size[j + 1])

        def away(j):
            if j == 0:
                return (1 - value[0]) * apart + offset
            return start[j] + (1 - value[j]) * size[j + 1]

        def rs(j):
            return remote(src.at[span(away(j), size[j + 1]), :], bufs[j],
                          rs_s.at[g, j], rs_r.at[g, j], {"row": partner[j]})

        def ag(j):
            if j == 0:
                mine = span(start[1], size[1])
            else:
                mine = span(start[j + 1], size[j + 1])
            return remote(dst.at[mine, :], dst.at[mine, :],
                          ag_s.at[g, j], ag_r.at[g, j], {"row": partner[j]})

        def add(j):
            rs(j).wait()
            mine = size[j + 1]
            piece = min(mine, 128)

            def body(i):
                here = span(start[j + 1] + i * piece, piece)
                src[here, :] = src[here, :] + bufs[j][span(i * piece, piece), :]
            loop(0, mine // piece, body)

        def event(i):
            if i == 0:
                rs(0).start()
            elif i < bits:
                add(i - 1)
                rs(i).start()
            elif i == bits:
                add(bits - 1)
                finish(start[bits], size[bits])
                ag(bits - 1).start()
            else:
                j = 2 * bits - i
                ag(j).wait()
                if j > 0:
                    ag(j - 1).start()
        return [functools.partial(event, i) for i in range(2 * bits + 1)]

    def finish_column(s, start, size):
        piece = min(size, width, 128)

        def body(i):
            at = start + i * piece
            block = lax.div(c * rows + at, width)
            here = span(at, piece)
            y[s, here, :] = sign_ref[s, block] * part[s, here, :]
        loop(0, size // piece, body)

    source = lax.div(r * n_cols, n_rows)
    own_start = r * depth - source * rows
    parts = [[k for k in range(CHUNKS) if (k * ch // strip) % 2 == h] for h in range(2)]

    def z_copy(s, k, src, way):
        sem = zl_s if way < 0 else zr_s
        return remote(src, low.at[s, chunk(k), :], sem.at[s, k], z_r.at[s, k],
                      left if way < 0 else right)

    def z_send(s, k, src):
        @pl.when((c <= source) & (c > 0))
        def _():
            z_copy(s, k, src, -1).start()

        @pl.when((c >= source) & (c < end))
        def _():
            z_copy(s, k, src, 1).start()

    def z_root(s, h):
        @pl.when(c == source)
        def _():
            for k in parts[h]:
                z_send(s, k, y.at[s, span(own_start + k * ch, ch), :])
            for k in parts[h]:
                low[s, chunk(k), :] = y[s, span(own_start + k * ch, ch), :]

    def z_relay(s, k):
        @pl.when(c != source)
        def _():
            z_copy(s, k, low.at[s, chunk(k), :], 1).wait_recv()
            z_send(s, k, low.at[s, chunk(k), :])

    def low_copy(s):
        return pltpu.make_async_copy(low.at[s], low_out.at[s], o_sem.at[s])

    tb = rows // 8

    def turn_copy(i):
        s, b = i // 8, i % 8
        return pltpu.make_async_copy(
            turned.at[i % 2], y_out.at[s, :, pl.ds(b * tb, tb)], t_sem.at[i % 2]
        )

    def turn(i):
        s, b = i // 8, i % 8
        if i >= 2:
            turn_copy(i - 2).wait()
        turned[i % 2] = y[s, pl.ds(b * tb, tb), :].T
        turn_copy(i).start()

    def inner(s, k):
        b = halves(bf[s, chunk(k), :].T)
        dpart[s] += dot3(b, halves(low[s, chunk(k), :]))

    barrier = pltpu.get_barrier_semaphore()
    for j in range(bits):
        pl.semaphore_signal(barrier, inc=1, device_id={"row": partner[j]}, device_id_type=MESH)

    @pl.when(c > 0)
    def _():
        pl.semaphore_signal(barrier, inc=1, device_id=left, device_id_type=MESH)

    @pl.when(c < end)
    def _():
        pl.semaphore_signal(barrier, inc=1, device_id=right, device_id_type=MESH)

    beside = lax.div(c + end - 1, end) + lax.div(2 * end - 1 - c, end)
    pl.semaphore_wait(barrier, bits + beside)

    a_copy(0)[2].start()
    dpart[...] = jnp.zeros_like(dpart)

    def column_events(s, h):
        g = 2 * s + h
        return reduce_events(g, part.at[s], [b.at[g] for b in rs_buf], y.at[s],
                             rows // 2, h * strip, strip, functools.partial(finish_column, s))

    def diag_events(s):
        def finish(start, size):
            here = span(start, size)
            dsum[s, here, :] = dpart[s, here, :]
        return reduce_events(4 + s, dpart.at[s], [b.at[s] for b in d_buf], dsum.at[s],
                             width // 2, 0, width // 2, finish)

    events = {(s, h): column_events(s, h) for s in range(2) for h in range(2)}
    root = {key: functools.partial(z_root, *key) for key in events}
    ready = CHUNKS + end
    quarter = TILES // 4

    loop(0, ready, panel_step)
    per = CHUNKS // 2 // 4
    for q in range(4):
        def both(i, q=q):
            panel_step(ready + q * per + i)
            each = quarter // per
            loop(0, each, lambda m: multiply(0, q * quarter + i * each + m))
        loop(0, per, both)
        e, f = events[0, 0], events[0, 1]
        for event in ([e[0]], [e[1]], [f[0]], [e[2], f[1]])[q]:
            event()
    steps = [functools.partial(panel_step, ready + 4 * per + i) for i in range(CHUNKS - 4 * per)]
    e, f = events[0, 0][3:] + [root[0, 0]], events[0, 1][2:] + [root[0, 1]]
    late = 2
    for step in weave(steps, weave(e, f[:-late])):
        step()
    order = parts[0] + parts[1]
    relays = [functools.partial(z_relay, 0, k) for k in order]
    for q in range(4):
        loop(0, quarter, lambda m: multiply(1, q * quarter + m))
        e, g = events[1, 0], events[1, 1]
        if q == 0:
            todo = f[-late:] + [e[0]]
        else:
            todo = relays[:2] + [[], [e[1]], [g[0]], [e[2], g[1]]][q]
            relays = relays[2:]
        for event in todo:
            event()
    e, g = events[1, 0][3:] + [root[1, 0]], events[1, 1][2:] + [root[1, 1]]
    for step in weave(weave(e, g), relays):
        step()
    low_copy(0).start()
    inners = [functools.partial(loop, i * CHUNKS // 4, (i + 1) * CHUNKS // 4,
                                lambda k: inner(0, k)) for i in range(4)]
    side = weave(inners + diag_events(0), [functools.partial(turn, i) for i in range(16)])

    def last(k):
        z_relay(1, k)
        inner(1, k)
    for step in weave([functools.partial(last, k) for k in order], side):
        step()
    low_copy(1).start()
    for event in diag_events(1):
        event()
    diag_out[...] = dinv_ref[...] - dsum[...]

    for s in range(2):
        def drain(k, s=s):
            @pl.when(c < end)
            def _():
                plus_copy(s, k).wait_send()

            @pl.when(c > 0)
            def _():
                minus_copy(s, k).wait_send()

            src = low.at[s, chunk(k), :]

            @pl.when((c <= source) & (c > 0))
            def _():
                z_copy(s, k, src, -1).wait_send()

            @pl.when((c >= source) & (c < end))
            def _():
                z_copy(s, k, src, 1).wait_send()
        loop(0, CHUNKS, drain)
    turn_copy(14).wait()
    turn_copy(15).wait()
    for s in range(2):
        low_copy(s).wait()


def exchange(n_rows, n_cols, a, panel, scale, sign, dinv):
    rows, depth = a.shape
    width = panel.shape[1]
    bits = n_rows.bit_length() - 1
    vmem = pl.BlockSpec(memory_space=pltpu.VMEM)
    smem = pl.BlockSpec(memory_space=pltpu.SMEM)
    anywhere = pl.BlockSpec(memory_space=pl.ANY)
    dma = pltpu.SemaphoreType.DMA
    n = CHUNKS
    return pl.pallas_call(
        functools.partial(kernel, n_rows, n_cols),
        out_shape=(
            jax.ShapeDtypeStruct((2, width, rows), F32),
            jax.ShapeDtypeStruct((2, depth, width), F32),
            jax.ShapeDtypeStruct((2, width, width), F32),
        ),
        in_specs=[anywhere, vmem, smem, smem, vmem],
        out_specs=(anywhere, anywhere, vmem),
        scratch_shapes=[
            pltpu.VMEM((2, depth, width), F32),
            pltpu.VMEM((2, depth, width), BF16),
            pltpu.VMEM((2, depth, width), BF16),
            pltpu.VMEM((2, depth, width), F32),
            pltpu.VMEM((2, depth, width), F32),
            pltpu.VMEM((2, rows, width), F32),
            pltpu.VMEM((2, rows, width), F32),
            pltpu.VMEM((2, depth, width), F32),
            pltpu.VMEM((2, rows // TILES, depth), F32),
            pltpu.VMEM((2, width, rows // 8), F32),
            pltpu.VMEM((2, width, width), F32),
            pltpu.VMEM((2, width, width), F32),
            *[pltpu.VMEM((4, rows // 4 >> j, width), F32) for j in range(bits)],
            *[pltpu.VMEM((2, width // 2 >> j, width), F32) for j in range(bits)],
            dma((2, n)), dma((2, n)), dma((2, n)), dma((2, n)),
            dma((6, bits)), dma((6, bits)), dma((6, bits)), dma((6, bits)),
            dma((2, n)), dma((2, n)), dma((2, n)),
            dma((2,)), dma((2,)), dma((2,)),
        ],
        compiler_params=pltpu.CompilerParams(
            collective_id=0, has_side_effects=True, vmem_limit_bytes=66_000_000
        ),
    )(a, panel, scale, sign, dinv)


def shards(inverse_rows, panels, diag_inverse, pattern, owner_slot):
    live = pattern.astype(F32)
    mine = (owner_slot == lax.axis_index("col")).astype(F32)
    y, low, diag = exchange(
        lax.axis_size("row"), lax.axis_size("col"), inverse_rows, panels[0],
        live * mine[:, None], -live, diag_inverse,
    )
    return low, y, diag


def solution(mesh):
    in_specs = (P("col", "row"), P("col", "row", None), P(), P(), P())
    out_specs = (P(None, "row", None), P(None, None, "col"), P())
    return jax.shard_map(shards, mesh=mesh, in_specs=in_specs, out_specs=out_specs, check_vma=False)
```

time: 382 us -> 311 us (0.81); the launches traced: 377 us -> 310 us
  Pallas kernels: 346 us -> 297 us
  other arithmetic: 12 us -> 1.97 us
  local copies, waits for them, and re-layouts: 17.1 us -> 10.3 us
    pallas_call x1, Pallas kernels: 346 us -> 297 us  [exchange(): pl.pallas_call(functools.partial(kernel, n_rows, n_cols), out_shape=(jax....]
    dynamic_slice x6 -> x0, local copies, waits for them, and re-layouts: 5.45 us -> none  [the longest x3 3.36 us: back(): lax.dynamic_index_in_dim(x, o, 0, keepdims=False)]
    unnamed x10 -> x7, local copies, waits for them, and re-layouts: 10.6 us -> 10.3 us
where the time goes in v2:
time: 311 us; the launch traced here: 310 us
  Pallas kernels  297 us (95%)
  local copies, waits for them, and re-layouts  10.3 us (3%)
    pallas_call x1, Pallas kernels, exchange(): pl.pallas_call(functools.partial(kernel, n_rows, n_cols), out_shape=(jax....  297 us
    unnamed x7, local copies, waits for them, and re-layouts  10.3 us

profile of v2, /device:TPU:7, one launch (start us, length us, event | category | flops | bytes accessed | tf_op | source)
XLA Modules:
  0.0 310.1 jit_solution(8460308282723435645)
XLA Ops:
  0.6 0.7 compare_convert_fusion
  1.3 1.3 convert_negate_fusion
  2.6 297.1 %shard_map.76 = (f32[2,256,4096]{2,1,0:T(8,128)}, f32[2,2048,256]{2,1,0:T(8,128)}, f32[2,256,256]{2,1,0:T(8,128)}) custom-call(f32[4096,2048]{1,0:T(8,128)} %a_ref.1, f32[2048,256]{1,0:T(8,128)} %bitcast.1, f32[2,64]{1,0:T(2,128)} %get-tuple-element.10.scale_ref, f32[2,64]{1,0:T(2,128)} %get-tuple-element.9.sign_ref, f32[2,256,256]{2,1,0:T(8,128)} %dinv_ref.1), custom_call_target="tpu_custom_call" | custom-call | tf_op jit(solution)/shard_map/pallas_call | solution.py:405
  299.7 0.0 copy-start
  299.7 4.8 %copy.11 = f32[2,2048,256]{2,1,0:T(8,128)} copy(f32[2,2048,256]{2,1,0:T(8,128)} %get-tuple-element.14) | data formatting | bytes 8388608
  304.5 1.4 copy-done
  305.9 0.0 copy-start.1
  305.9 3.4 %copy.12 = f32[2,256,4096]{2,1,0:T(8,128)} copy(f32[2,256,4096]{2,1,0:T(8,128)S(1)} %copy-done) | data formatting | bytes 16777216
  309.3 0.0 copy-done.1
  309.3 0.8 copy.13
Async XLA Ops:
  299.7 6.2 %copy-start = (f32[2,256,4096]{2,1,0:T(8,128)S(1)}, f32[2,256,4096]{2,1,0:T(8,128)}, u32[]{:S(2)}) copy-start(f32[2,256,4096]{2,1,0:T(8,128)} %get-tuple-element.15) | copy-start | bytes 25165828
  305.9 3.4 %copy-start.1 = (f32[2,256,256]{2,1,0:T(8,128)S(1)}, f32[2,256,256]{2,1,0:T(8,128)}, u32[]{:S(2)}) copy-start(f32[2,256,256]{2,1,0:T(8,128)} %get-tuple-element.16) | copy-start | bytes 1572868

commit v3 on v2

--- a/solution.py
+++ b/solution.py
@@ -12,6 +12,7 @@
 BF16 = jnp.bfloat16
 CHUNKS = 16
 TILES = 16
+AHEAD = 3
 
 
 def halves(x):
@@ -123,7 +124,7 @@
     total_chunks = 2 * CHUNKS
 
     def panel_step(j):
-        up = j - c
+        up = j - AHEAD * c
 
         @pl.when((up >= 0) & (up < total_chunks))
         def _():
@@ -142,7 +143,7 @@
             def _():
                 plus_copy(s, k).start()
 
-        down = j - (end - c)
+        down = j - AHEAD * (end - c)
 
         @pl.when((down >= 0) & (down < total_chunks))
         def _():
@@ -161,7 +162,7 @@
             def _():
                 minus_copy(s, k).start()
 
-        at = j - end
+        at = j - AHEAD * end
 
         @pl.when(at >= 0)
         def _():
@@ -318,7 +319,7 @@
 
     events = {(s, h): column_events(s, h) for s in range(2) for h in range(2)}
     root = {key: functools.partial(z_root, *key) for key in events}
-    ready = CHUNKS + end
+    ready = CHUNKS + AHEAD * end
     quarter = TILES // 4
 
     loop(0, ready, panel_step)

time: 311 us -> 289 us (0.929)
  Pallas kernels: 297 us -> 276 us
    pallas_call x1, Pallas kernels: 297 us -> 276 us  [exchange(): pl.pallas_call(functools.partial(kernel, n_rows, n_cols), out_shape=(jax....]
where the time goes in v3:
time: 289 us
  Pallas kernels  276 us (96%)
  local copies, waits for them, and re-layouts  10.3 us (4%)
    pallas_call x1, Pallas kernels, exchange(): pl.pallas_call(functools.partial(kernel, n_rows, n_cols), out_shape=(jax....  276 us
    unnamed x7, local copies, waits for them, and re-layouts  10.3 us

profile of v3, /device:TPU:7, one launch (start us, length us, event | category | flops | bytes accessed | tf_op | source)
XLA Modules:
  0.0 288.8 jit_solution(8235958050368429128)
XLA Ops:
  0.6 0.7 compare_convert_fusion
  1.3 1.3 convert_negate_fusion
  2.6 275.9 %shard_map.76 = (f32[2,256,4096]{2,1,0:T(8,128)}, f32[2,2048,256]{2,1,0:T(8,128)}, f32[2,256,256]{2,1,0:T(8,128)}) custom-call(f32[4096,2048]{1,0:T(8,128)} %a_ref.1, f32[2048,256]{1,0:T(8,128)} %bitcast.1, f32[2,64]{1,0:T(2,128)} %get-tuple-element.10.scale_ref, f32[2,64]{1,0:T(2,128)} %get-tuple-element.9.sign_ref, f32[2,256,256]{2,1,0:T(8,128)} %dinv_ref.1), custom_call_target="tpu_custom_call" | custom-call | tf_op jit(solution)/shard_map/pallas_call | solution.py:406
  278.5 0.0 copy-start
  278.5 4.8 %copy.11 = f32[2,2048,256]{2,1,0:T(8,128)} copy(f32[2,2048,256]{2,1,0:T(8,128)} %get-tuple-element.14) | data formatting | bytes 8388608
  283.2 1.4 copy-done
  284.6 0.0 copy-start.1
  284.6 3.4 %copy.12 = f32[2,256,4096]{2,1,0:T(8,128)} copy(f32[2,256,4096]{2,1,0:T(8,128)S(1)} %copy-done) | data formatting | bytes 16777216
  288.0 0.0 copy-done.1
  288.0 0.8 copy.13
Async XLA Ops:
  278.5 6.2 %copy-start = (f32[2,256,4096]{2,1,0:T(8,128)S(1)}, f32[2,256,4096]{2,1,0:T(8,128)}, u32[]{:S(2)}) copy-start(f32[2,256,4096]{2,1,0:T(8,128)} %get-tuple-element.15) | copy-start | bytes 25165828
  284.6 3.4 %copy-start.1 = (f32[2,256,256]{2,1,0:T(8,128)S(1)}, f32[2,256,256]{2,1,0:T(8,128)}, u32[]{:S(2)}) copy-start(f32[2,256,256]{2,1,0:T(8,128)} %get-tuple-element.16) | copy-start | bytes 1572868
